TPU v7x, 32 devices: a whole 2x2x4 slice. The times are simulated.
32 devices in a mesh: bx: 4 (over y, x), by: 8 (over z, core).
Axes of the slice: x: 2, y: 2, z: 4, core: 2. Of those that a mesh axis runs over, the one named last changes fastest.
Arguments:
- cells_in: float32 [128, 5, 4096], P(('bx', 'by')), may hold values from -0.5 to 2, as said below
- block_levels: int32 [128], P(('bx', 'by')), may hold values from 0 to 2
- send_x: int32 [32, 1], P(('bx', 'by')), may hold values from 0 to 3, as said below
- send_y: int32 [32, 1], P(('bx', 'by')), may hold values from 0 to 3, as said below
- layout: int32 [32, 3], P(('bx', 'by')), may hold values from -1 to 5, as said below
- face_out: int32 [32, 4, 4], P(('bx', 'by')), may hold values from 0 to 23, as said below
- ghost_src: int32 [32, 4, 6], P(('bx', 'by')), may hold values from 0 to 39
Outputs:
- cells_out: float32 [96, 5, 4096], P(('bx', 'by'))
Inputs may be any that keep to these rules, and one draw needn't show every extreme that they name: `cells_in`: fields 0 and 4 (density, pressure) lie in 1 to 2, fields 1 to 3 (velocities) in -0.5 to 0.5. Per device, send_x and send_y together name 2 distinct slots. Per device, send_x and send_y together name 2 distinct slots. `layout`: each device's codes name each of 4 to 5 once, at most 1 distinct own slots that neither send list names, and -1 for empty slots; some device keeps 1 own slots and some keeps none. `face_out`: entries are face numbers slot * 6 + face of the sending device, distinct within one device and direction.
All inputs are finite; a program needn't handle non-finite values.
Results may differ from a plain program's by a relative error of at most 0.0003.
Values sent between devices are 32-bit elements; how exact they have to be, the bound alone decides.
A program may use at most 64 MiB of HBM per device.

v0:
```python
import functools

import jax
import jax.numpy as jnp
from jax import lax
from jax.experimental import pallas as pl
from jax.experimental.pallas import tpu as pltpu
from jax.sharding import PartitionSpec as P

B = 16
FIELDS = 5
LANES = 128
HALVES = B * B // LANES
STRETCH = (B + 4) * 8
PLANE = 8
FACE = FIELDS * 2 * HALVES
FACE_ROOM = -(-FACE // 8) * 8
ROWS = B * B * B // LANES
BLOCK = FIELDS * ROWS
MESH = pl.DeviceIdType.MESH

gamma_gas = 1.4
step_base = 0.05


def choose(mask, a, b):
    if a is None and b is None:
        return None
    return jnp.where(mask, 0.0 if a is None else a, 0.0 if b is None else b)


def roll(value, shift, axis):
    size = (8, LANES)[axis]
    if value is None or shift % size == 0:
        return value
    return pltpu.roll(value, shift % size, axis)


def swap_lanes(planes, unit, lane):
    count = len(planes)
    planes = [roll(p, n * unit, 1) for n, p in enumerate(planes)]
    planes = [planes[-n % count] for n in range(count)]
    step = 1
    while step < count:
        mask = (lane & (step * unit)) != 0
        planes = [choose(mask, planes[(n - step) % count], planes[n]) for n in range(count)]
        step *= 2
    return [roll(p, -n * unit, 1) for n, p in enumerate(planes)]


def swap_xy(planes, coords):
    high = coords[0] >= PLANE // HALVES
    count = len(planes) // HALVES
    first = swap_lanes(planes[:count], B, coords[1])
    second = swap_lanes(planes[count:], B, coords[1])
    moved = [roll(choose(high, a, c), PLANE // HALVES, 0) for a, c in zip(first, second)]
    first = [choose(high, m, a) for m, a in zip(moved, first)]
    second = [choose(high, c, m) for m, c in zip(moved, second)]
    return first + second


def swap_yz(planes, coords):
    return swap_lanes(planes, 1, coords[1])


def plus(a, b):
    return b if a is None else a if b is None else a + b


def minmod(a, b):
    return jnp.maximum(jnp.minimum(a, b), 0.0) + jnp.minimum(jnp.maximum(a, b), 0.0)


def face_values(before, centre, after, half_ratio):
    s = [minmod(c - b, a - c) for b, c, a in zip(before, centre, after)]
    rho, un, _, _, p = centre
    advance = [
        un * s[0] + rho * s[1],
        un * s[1] + s[4] / rho,
        un * s[2],
        un * s[3],
        un * s[4] + gamma_gas * p * s[1],
    ]
    middle = [c - half_ratio * a for c, a in zip(centre, advance)]
    half = [0.5 * v for v in s]
    lower = [m - h for m, h in zip(middle, half)]
    upper = [m + h for m, h in zip(middle, half)]
    return lower, upper


def conserved(state):
    rho, un, u1, u2, p = state
    mn, m1, m2 = rho * un, rho * u1, rho * u2
    energy = p * (1.0 / (gamma_gas - 1.0)) + 0.5 * (mn * un + m1 * u1 + m2 * u2)
    return [rho, mn, m1, m2, energy]


def euler(state):
    rho, un, u1, u2, p = state
    cons = conserved(state)
    mn, energy = cons[1], cons[4]
    flux = [mn, mn * un + p, mn * u1, mn * u2, un * (energy + p)]
    elastic = gamma_gas * p
    signal = jnp.abs(un) + elastic * lax.rsqrt(elastic * rho)
    return flux, cons, signal


def face_flux(left, right):
    fa, ua, sa = euler(left)
    fb, ub, sb = euler(right)
    half_speed = 0.5 * jnp.maximum(sa, sb)
    return [0.5 * (f + g) - half_speed * (v - u) for f, g, u, v in zip(fa, fb, ua, ub)]


def kernel(
    slots, gmax, moves, cap_out,
    cells, levels_in, send_x_in, send_y_in, layout_in, face_out_in, ghost_src_in,
    out,
    ext, flux, partial, local_faces, far_faces, send_faces, ghosts, own, received, send_blocks, chosen,
    levels, send_x, send_y, layout, face_out, ghost_src,
    face_send, face_recv, block_send, block_recv, cell_sem, small_sem,
):
    cell_copies = [
        pltpu.make_async_copy(
            cells.at[f], ext.at[pl.ds(f * STRETCH + 2 * PLANE, B * PLANE)], cell_sem.at[f]
        )
        for f in range(FIELDS)
    ]
    small = (
        (face_out_in, face_out), (levels_in, levels), (ghost_src_in, ghost_src),
        (send_x_in, send_x), (send_y_in, send_y), (layout_in, layout),
    )
    small_copies = [
        pltpu.make_async_copy(source, target, small_sem.at[i])
        for i, (source, target) in enumerate(small)
    ]
    for copy in cell_copies + small_copies:
        copy.start()
    n_x, n_y = lax.axis_size("bx"), lax.axis_size("by")
    i_x, i_y = lax.axis_index("bx"), lax.axis_index("by")
    beside = (
        {"bx": lax.rem(i_x + 1, n_x)},
        {"bx": lax.rem(i_x + n_x - 1, n_x)},
        {"by": lax.rem(i_y + 1, n_y)},
        {"by": lax.rem(i_y + n_y - 1, n_y)},
    )
    partners = (
        {"bx": lax.rem(i_x + n_x // 2, n_x)},
        {"by": lax.rem(i_y + n_y // 2, n_y)},
    )
    barrier = pltpu.get_barrier_semaphore()
    for device in beside + partners:
        pl.semaphore_signal(barrier, inc=1, device_id=device, device_id_type=MESH)

    coords = [lax.broadcasted_iota(jnp.int32, (8, LANES), axis) for axis in (0, 1)]
    def row(plane):
        return pl.ds(plane * PLANE, PLANE)

    def ext_row(axis, field, plane):
        start = (axis * FIELDS + field) * STRETCH + plane * PLANE
        return pl.ds(pl.multiple_of(start, PLANE), PLANE)

    for field in range(FIELDS):
        cell_copies[field].wait()
        planes = [ext[ext_row(0, field, x + 2), :] for x in range(B)]
        planes = swap_xy(planes, coords)
        for y in range(B):
            ext[ext_row(1, field, y + 2), :] = planes[y]
        planes = swap_yz(planes, coords)
        for z in range(B):
            ext[ext_row(2, field, z + 2), :] = planes[z]

    face_lines = local_faces.reshape(6 * slots * FACE_ROOM, LANES)
    own_lines = own.reshape(slots * BLOCK, LANES)
    for axis in range(3):
        for side in range(2):
            for layer in range(2):
                plane = 2 + layer if side == 0 else B + 1 - layer
                for field in range(FIELDS):
                    for half in range(HALVES):
                        source = (axis * FIELDS + field) * STRETCH + plane * PLANE + half * slots
                        target = (axis * 2 + side) * FACE_ROOM + field * 4 + layer * 2 + half
                        face_lines[pl.ds(target, slots, stride=6 * FACE_ROOM), :] = ext[
                            pl.ds(source, slots), :
                        ]

    def local_face(code):
        return local_faces[code][:FACE]

    def own_rows(slot, first, count):
        return own[slot][first : first + count]

    small_copies[0].wait()
    for d in range(4):
        for k in range(gmax):
            send_faces[d, k] = local_face(face_out[0, d, k])

    pl.semaphore_wait(barrier, 6)
    face_copies = [
        pltpu.make_async_remote_copy(
            src_ref=send_faces.at[d],
            dst_ref=far_faces.at[pl.ds(d * gmax, gmax)],
            send_sem=face_send.at[d],
            recv_sem=face_recv.at[d],
            device_id=beside[d],
            device_id_type=MESH,
        )
        for d in range(4)
    ]
    for copy in face_copies:
        copy.start()

    for copy in small_copies[1:]:
        copy.wait()
    slot_of = lax.rem(coords[0], slots)
    level = jnp.zeros((8, LANES), jnp.int32)
    for b in range(slots):
        level = jnp.where(slot_of == b, levels[b], level)
    ratio = step_base * jnp.exp2(level.astype(jnp.float32))
    half_ratio = 0.5 * ratio

    def order(axis):
        return (
            0,
            1 + axis,
            1 + lax.rem(axis + 1, 3),
            1 + lax.rem(axis + 2, 3),
            4,
        )

    def sweep(axis, first, last):
        fields = order(axis)
        load = lambda plane: [ext[ext_row(axis, f, plane), :] for f in fields]
        before, centre = load(first - 1), load(first)
        left = None
        for plane in range(first, last + 1):
            after = load(plane + 1)
            lower, upper = face_values(before, centre, after, half_ratio)
            if left is not None:
                for f, value in zip(fields, face_flux(left, lower)):
                    flux[axis, f, row(plane - 2), :] = value
            left = upper
            before, centre = centre, after

    def inner(axis, carry):
        sweep(axis, 3, B)
        return carry

    lax.fori_loop(0, 3, inner, 0)

    def change(axis, field, faces):
        values = {i: flux[axis, field, row(i), :] for i in faces}
        after = [values.get(i + 1) for i in range(B)]
        before = [values.get(i) for i in range(B)]
        return [plus(a, None if b is None else -b) for a, b in zip(after, before)]

    def changes(field, faces):
        planes = swap_yz(change(2, field, faces), coords)
        planes = [plus(a, c) for a, c in zip(planes, change(1, field, faces))]
        planes = swap_xy(planes, coords)
        return [plus(a, c) for a, c in zip(planes, change(0, field, faces))]

    for x in range(B):
        initial = conserved([ext[ext_row(0, f, x + 2), :] for f in range(FIELDS)])
        for field in range(FIELDS):
            partial[field, row(x), :] = initial[field]
    for field in range(FIELDS):
        planes = changes(field, range(2, B - 1))
        for x in range(B):
            partial[field, row(x), :] = partial[field, row(x), :] - ratio * planes[x]

    for copy in face_copies:
        copy.wait()

    for axis in range(3):
        for side in range(2):
            for b in range(slots):
                code = ghost_src[0, b, axis * 2 + side]
                near = local_face(jnp.minimum(code, 6 * slots - 1))
                far = far_faces[jnp.maximum(code - 6 * slots, 0)]
                ghost = b * 6 + axis * 2 + side
                ghosts[ghost] = jnp.where(code < 6 * slots, near, far)
                for layer in range(2):
                    plane = 1 - layer if side == 0 else B + 2 + layer
                    for half in range(HALVES):
                        start = axis * FIELDS * STRETCH + plane * PLANE + half * slots + b
                        ext[pl.ds(start, FIELDS, stride=STRETCH), :] = ghosts[
                            ghost, pl.ds(layer * 2 + half, FIELDS, stride=4), :
                        ]

    def outer(axis, carry):
        sweep(axis, 1, 3)
        sweep(axis, B, B + 2)
        return carry

    lax.fori_loop(0, 3, outer, 0)

    block_copies = []
    for field in range(FIELDS):
        planes = changes(field, (0, 1, B - 1, B))
        for x in range(B):
            value = partial[field, row(x), :] - ratio * planes[x]
            for half in range(HALVES):
                own_lines[pl.ds(field * ROWS + x * HALVES + half, slots, stride=BLOCK), :] = value[
                    half * slots : (half + 1) * slots
                ]
        for t, listed in enumerate((send_x, send_y)):
            rows = pl.ds(field * ROWS, ROWS)
            for m in range(moves):
                send_blocks[t, m, rows, :] = own_rows(listed[0, m], field * ROWS, ROWS)
            copy = pltpu.make_async_remote_copy(
                src_ref=send_blocks.at[t, :, rows],
                dst_ref=received.at[pl.ds(t * moves, moves), rows],
                send_sem=block_send.at[t, field],
                recv_sem=block_recv.at[t, field],
                device_id=partners[t],
                device_id_type=MESH,
            )
            copy.start()
            block_copies.append((t, field, copy))

    for j in range(cap_out):
        code = layout[0, j]
        value = own_rows(jnp.clip(code, 0, slots - 1), 0, BLOCK)
        chosen[pl.ds(j * BLOCK, BLOCK), :] = jnp.where(code < 0, 0.0, value)
    for field in range(FIELDS):
        for k in range(ROWS):
            out[field, :, pl.ds(k * LANES, LANES)] = chosen[
                pl.ds(field * ROWS + k, cap_out, stride=BLOCK), :
            ]
    slot_row = lax.broadcasted_iota(jnp.int32, (cap_out, LANES), 0)
    code_row = jnp.zeros((cap_out, LANES), jnp.int32)
    for j in range(cap_out):
        code_row = jnp.where(slot_row == j, layout[0, j], code_row)
    for t, field, copy in block_copies:
        copy.wait()
        for m in range(moves):
            arrived = t * moves + m
            here = code_row == slots + arrived
            for k in range(ROWS):
                at = (field, slice(None), pl.ds(k * LANES, LANES))
                line = received[arrived, pl.ds(field * ROWS + k, 1), :]
                out[at] = jnp.where(here, jnp.broadcast_to(line, here.shape), out[at])


def on_device(cells_in, block_levels, send_x, send_y, layout, face_out, ghost_src):
    slots = cells_in.shape[0]
    gmax = face_out.shape[2]
    moves = send_x.shape[1]
    cap_out = layout.shape[1]
    small = (block_levels, send_x, send_y, layout, face_out, ghost_src)
    anywhere = pl.BlockSpec(memory_space=pltpu.HBM)
    lines = cells_in.reshape(slots, FIELDS, ROWS, LANES).transpose(1, 2, 0, 3)
    lines = lines.reshape(FIELDS, ROWS * slots, LANES)
    table = functools.partial(pltpu.VMEM, dtype=jnp.float32)
    out = pl.pallas_call(
        functools.partial(kernel, slots, gmax, moves, cap_out),
        out_shape=pltpu.VMEM((FIELDS, cap_out, cells_in.shape[2]), jnp.float32),
        in_specs=[anywhere] * 7,
        out_specs=pl.BlockSpec(memory_space=pltpu.VMEM),
        scratch_shapes=[
            table((3 * FIELDS * STRETCH, LANES)),
            table((3, FIELDS, (B + 1) * PLANE, LANES)),
            table((FIELDS, B * PLANE, LANES)),
            table((6 * slots, FACE_ROOM, LANES)),
            table((4 * gmax, FACE, LANES)),
            table((4, gmax, FACE, LANES)),
            table((6 * slots, FACE, LANES)),
            table((slots, BLOCK, LANES)),
            table((2 * moves, BLOCK, LANES)),
            table((2, moves, BLOCK, LANES)),
            table((cap_out * BLOCK, LANES)),
            *(pltpu.SMEM(a.shape, jnp.int32) for a in small),
            pltpu.SemaphoreType.DMA((4,)),
            pltpu.SemaphoreType.DMA((4,)),
            pltpu.SemaphoreType.DMA((2, FIELDS)),
            pltpu.SemaphoreType.DMA((2, FIELDS)),
            pltpu.SemaphoreType.DMA((FIELDS,)),
            pltpu.SemaphoreType.DMA((len(small),)),
        ],
        compiler_params=pltpu.CompilerParams(collective_id=0, has_side_effects=True),
        name="section",
    )(lines, *small)
    return out.transpose(1, 0, 2)


def solution(mesh):
    return jax.shard_map(
        on_device,
        mesh=mesh,
        in_specs=(
            P(("bx", "by"), None, None),
            P(("bx", "by")),
            P(("bx", "by"), None),
            P(("bx", "by"), None),
            P(("bx", "by"), None),
            P(("bx", "by"), None, None),
            P(("bx", "by"), None, None),
        ),
        out_specs=P(("bx", "by"), None, None),
        check_vma=False,
    )
```

profile of v0, /device:TPU:0, one launch (start us, length us, event | category | flops | bytes accessed | tf_op | source)
XLA Modules:
  0.0 17.9 jit_solution(6621776631560685514)
XLA Ops:
  1.3 15.9 %section.1 = f32[5,3,4096]{2,1,0:T(4,128)S(1)} custom-call(f32[5,128,128]{2,1,0:T(8,128)} %bitcast.7, s32[4]{0:T(128)} %levels_in.1, s32[1,1]{1,0:T(1,128)S(6)} %copy.11.send_x_in, s32[1,1]{1,0:T(1,128)S(6)} %copy.12.send_y_in, s32[1,3]{1,0:T(1,128)} %layout_in.1, s32[1,4,4]{2,1,0:T(4,128)} %face_out_in.1, s32[1,4,6]{2,1,0:T(4,128)} %ghost_src_in.1), custom_call_target="tpu_custom_call" | custom-call | tf_op jit(solution)/shard_map/section/pallas_call | solution.py:356
  17.2 0.7 %copy.10 = f32[3,5,4096]{2,0,1:T(4,128)} copy(f32[3,5,4096]{2,0,1:T(4,128)S(1)} %bitcast.6) | data formatting | bytes 491520
where the time goes:
time: 18.1 us; the launch traced here: 17.9 us
  Pallas kernels  15.9 us (88%)
  between operations  1.3 us (7%)
  local copies, waits for them, and re-layouts  0.73 us (4%)
    pallas_call x1, Pallas kernels, on_device(): pl.pallas_call(functools.partial(kernel, slots, gmax, moves, cap_out), ou...  15.9 us
    unnamed x1, local copies, waits for them, and re-layouts  0.73 us

commit v1 on v0

--- a/solution.py
+++ b/solution.py
@@ -17,7 +17,15 @@
 FACE_ROOM = -(-FACE // 8) * 8
 ROWS = B * B * B // LANES
 BLOCK = FIELDS * ROWS
+INNER = B - 4
 MESH = pl.DeviceIdType.MESH
+
+SWAPS = (
+    (20, ((14, 4), (30, 4), (46, 4), (62, 4), (78, 4), (94, 12))),
+    (60, ((106, 8),)),
+    (68, ((114, 8),)),
+    (76, ((122, 8),)),
+)
 
 gamma_gas = 1.4
 step_base = 0.05
@@ -116,9 +124,10 @@
     slots, gmax, moves, cap_out,
     cells, levels_in, send_x_in, send_y_in, layout_in, face_out_in, ghost_src_in,
     out,
-    ext, flux, partial, local_faces, far_faces, send_faces, ghosts, own, received, send_blocks, chosen,
+    edge, local_faces, far_faces, send_faces, ghosts, ext, flux, total,
+    early_out, early_in, late_out, late_in, arrived,
     levels, send_x, send_y, layout, face_out, ghost_src,
-    face_send, face_recv, block_send, block_recv, cell_sem, small_sem,
+    face_send, face_recv, early_send, early_recv, late_send, late_recv, cell_sem, small_sem,
 ):
     cell_copies = [
         pltpu.make_async_copy(
@@ -153,6 +162,7 @@
         pl.semaphore_signal(barrier, inc=1, device_id=device, device_id_type=MESH)
 
     coords = [lax.broadcasted_iota(jnp.int32, (8, LANES), axis) for axis in (0, 1)]
+
     def row(plane):
         return pl.ds(plane * PLANE, PLANE)
 
@@ -160,35 +170,36 @@
         start = (axis * FIELDS + field) * STRETCH + plane * PLANE
         return pl.ds(pl.multiple_of(start, PLANE), PLANE)
 
+    for copy in cell_copies:
+        copy.wait()
+    rim = (0, 1, B - 2, B - 1)
     for field in range(FIELDS):
-        cell_copies[field].wait()
         planes = [ext[ext_row(0, field, x + 2), :] for x in range(B)]
         planes = swap_xy(planes, coords)
-        for y in range(B):
-            ext[ext_row(1, field, y + 2), :] = planes[y]
+        for i, y in enumerate(rim):
+            edge[row(field * 4 + i), :] = planes[y]
         planes = swap_yz(planes, coords)
-        for z in range(B):
-            ext[ext_row(2, field, z + 2), :] = planes[z]
+        for i, z in enumerate(rim):
+            edge[row((FIELDS + field) * 4 + i), :] = planes[z]
 
     face_lines = local_faces.reshape(6 * slots * FACE_ROOM, LANES)
-    own_lines = own.reshape(slots * BLOCK, LANES)
     for axis in range(3):
         for side in range(2):
             for layer in range(2):
-                plane = 2 + layer if side == 0 else B + 1 - layer
+                nth = layer if side == 0 else 3 - layer
                 for field in range(FIELDS):
                     for half in range(HALVES):
-                        source = (axis * FIELDS + field) * STRETCH + plane * PLANE + half * slots
                         target = (axis * 2 + side) * FACE_ROOM + field * 4 + layer * 2 + half
-                        face_lines[pl.ds(target, slots, stride=6 * FACE_ROOM), :] = ext[
-                            pl.ds(source, slots), :
-                        ]
+                        if axis == 0:
+                            at = field * STRETCH + (rim[nth] + 2) * PLANE + half * slots
+                            value = ext[pl.ds(at, slots), :]
+                        else:
+                            at = (((axis - 1) * FIELDS + field) * 4 + nth) * PLANE + half * slots
+                            value = edge[pl.ds(at, slots), :]
+                        face_lines[pl.ds(target, slots, stride=6 * FACE_ROOM), :] = value
 
     def local_face(code):
         return local_faces[code][:FACE]
-
-    def own_rows(slot, first, count):
-        return own[slot][first : first + count]
 
     small_copies[0].wait()
     for d in range(4):
@@ -209,6 +220,14 @@
     ]
     for copy in face_copies:
         copy.start()
+    for field in range(FIELDS):
+        planes = [ext[ext_row(0, field, x + 2), :] for x in range(B)]
+        planes = swap_xy(planes, coords)
+        for y in range(B):
+            ext[ext_row(1, field, y + 2), :] = planes[y]
+        planes = swap_yz(planes, coords)
+        for z in range(B):
+            ext[ext_row(2, field, z + 2), :] = planes[z]
 
     for copy in small_copies[1:]:
         copy.wait()
@@ -260,18 +279,66 @@
         planes = swap_xy(planes, coords)
         return [plus(a, c) for a, c in zip(planes, change(0, field, faces))]
 
+    def total_row(field, x):
+        return row(field * B + x)
+
     for x in range(B):
         initial = conserved([ext[ext_row(0, f, x + 2), :] for f in range(FIELDS)])
         for field in range(FIELDS):
-            partial[field, row(x), :] = initial[field]
+            total[total_row(field, x), :] = initial[field]
     for field in range(FIELDS):
         planes = changes(field, range(2, B - 1))
         for x in range(B):
-            partial[field, row(x), :] = partial[field, row(x), :] - ratio * planes[x]
+            total[total_row(field, x), :] = total[total_row(field, x), :] - ratio * planes[x]
+
+    lane = lax.broadcasted_iota(jnp.int32, (INNER, LANES), 1)
+
+    def any_of(spans):
+        found = None
+        for start, stop in spans:
+            test = (lane >= start) & (lane < stop)
+            found = test if found is None else found | test
+        return found
+
+    into = [any_of([((a + shift) % LANES, (a + shift) % LANES + n) for a, n in spans]) for shift, spans in SWAPS]
+    outof = [
+        any_of([span for a, n in spans for span in ((a, min(a + n, LANES)), (0, a + n - LANES)) if span[1] > span[0]])
+        for shift, spans in SWAPS
+    ]
+
+    def exchanged(kept, other, masks, sign):
+        for (shift, _), mask in zip(SWAPS, masks):
+            kept = jnp.where(mask, pltpu.roll(other, (sign * shift) % LANES, 1), kept)
+        return kept
+
+    def half_lines(slot, field, half):
+        return total[pl.ds((field * B + 2) * PLANE + half * slots + slot, INNER, stride=PLANE), :]
+
+    def edge_lines(slot, field, x):
+        return total[pl.ds((field * B + x) * PLANE + slot, 2 * HALVES, stride=slots), :]
+
+    lists = [(t, m, listed[0, m]) for t, listed in enumerate((send_x, send_y)) for m in range(moves)]
+
+    def to_partner(t, source, target, send_sem, recv_sem):
+        return pltpu.make_async_remote_copy(
+            src_ref=source.at[t],
+            dst_ref=target.at[t],
+            send_sem=send_sem.at[t],
+            recv_sem=recv_sem.at[t],
+            device_id=partners[t],
+            device_id_type=MESH,
+        )
+
+    for t, m, slot in lists:
+        for field in range(FIELDS):
+            first, second = (half_lines(slot, field, half) for half in range(HALVES))
+            early_out[t, m, pl.ds(field * INNER, INNER), :] = exchanged(second, first, outof, -1)
+    early_copies = [to_partner(t, early_out, early_in, early_send, early_recv) for t in range(2)]
+    for copy in reversed(early_copies):
+        copy.start()
 
     for copy in face_copies:
         copy.wait()
-
     for axis in range(3):
         for side in range(2):
             for b in range(slots):
@@ -295,52 +362,62 @@
 
     lax.fori_loop(0, 3, outer, 0)
 
-    block_copies = []
     for field in range(FIELDS):
         planes = changes(field, (0, 1, B - 1, B))
         for x in range(B):
-            value = partial[field, row(x), :] - ratio * planes[x]
-            for half in range(HALVES):
-                own_lines[pl.ds(field * ROWS + x * HALVES + half, slots, stride=BLOCK), :] = value[
-                    half * slots : (half + 1) * slots
-                ]
-        for t, listed in enumerate((send_x, send_y)):
-            rows = pl.ds(field * ROWS, ROWS)
-            for m in range(moves):
-                send_blocks[t, m, rows, :] = own_rows(listed[0, m], field * ROWS, ROWS)
-            copy = pltpu.make_async_remote_copy(
-                src_ref=send_blocks.at[t, :, rows],
-                dst_ref=received.at[pl.ds(t * moves, moves), rows],
-                send_sem=block_send.at[t, field],
-                recv_sem=block_recv.at[t, field],
-                device_id=partners[t],
-                device_id_type=MESH,
-            )
-            copy.start()
-            block_copies.append((t, field, copy))
+            total[total_row(field, x), :] = total[total_row(field, x), :] - ratio * planes[x]
+
+    for t, m, slot in reversed(lists):
+        for field in range(FIELDS):
+            first, second = (half_lines(slot, field, half) for half in range(HALVES))
+            late_out[t, m, pl.ds(field * INNER, INNER), :] = exchanged(first, second, into, 1)
+            for i, x in enumerate((0, B - 2)):
+                at = FIELDS * INNER + field * 8 + i * 4
+                late_out[t, m, pl.ds(at, 4), :] = edge_lines(slot, field, x)
+    to_x, to_y = (to_partner(t, late_out, late_in, late_send, late_recv) for t in range(2))
+    yields = i_y >= n_y - n_y // 4
+
+    @pl.when(jnp.logical_not(yields))
+    def _():
+        to_y.start()
+        to_x.start()
+
+    @pl.when(yields)
+    def _():
+        to_x.start()
+        to_x.wait_send()
+        to_y.start()
+
+    for t in range(2):
+        early_copies[t].wait()
+    for t in range(2):
+        (to_x, to_y)[t].wait_recv()
+        for m in range(moves):
+            block = t * moves + m
+            for field in range(FIELDS):
+                early = early_in[t, m, pl.ds(field * INNER, INNER), :]
+                late = late_in[t, m, pl.ds(field * INNER, INNER), :]
+                at = field * ROWS + 2 * HALVES
+                arrived[block, pl.ds(at, INNER, stride=HALVES), :] = exchanged(late, early, into, 1)
+                arrived[block, pl.ds(at + 1, INNER, stride=HALVES), :] = exchanged(early, late, outof, -1)
+                for i, x in enumerate((0, B - 2)):
+                    at = FIELDS * INNER + field * 8 + i * 4
+                    arrived[block, pl.ds(field * ROWS + x * HALVES, 4), :] = late_in[t, m, pl.ds(at, 4), :]
 
     for j in range(cap_out):
         code = layout[0, j]
-        value = own_rows(jnp.clip(code, 0, slots - 1), 0, BLOCK)
-        chosen[pl.ds(j * BLOCK, BLOCK), :] = jnp.where(code < 0, 0.0, value)
-    for field in range(FIELDS):
-        for k in range(ROWS):
-            out[field, :, pl.ds(k * LANES, LANES)] = chosen[
-                pl.ds(field * ROWS + k, cap_out, stride=BLOCK), :
-            ]
-    slot_row = lax.broadcasted_iota(jnp.int32, (cap_out, LANES), 0)
-    code_row = jnp.zeros((cap_out, LANES), jnp.int32)
-    for j in range(cap_out):
-        code_row = jnp.where(slot_row == j, layout[0, j], code_row)
-    for t, field, copy in block_copies:
-        copy.wait()
-        for m in range(moves):
-            arrived = t * moves + m
-            here = code_row == slots + arrived
-            for k in range(ROWS):
-                at = (field, slice(None), pl.ds(k * LANES, LANES))
-                line = received[arrived, pl.ds(field * ROWS + k, 1), :]
-                out[at] = jnp.where(here, jnp.broadcast_to(line, here.shape), out[at])
+        mine = jnp.clip(code, 0, slots - 1)
+        theirs = jnp.clip(code - slots, 0, 2 * moves - 1)
+        for k in range(0, BLOCK, PLANE):
+            own = total[pl.ds(mine + k * slots, PLANE, stride=slots), :]
+            value = jnp.where(code < slots, own, arrived[theirs, pl.ds(k, PLANE), :])
+            out[pl.ds(k * slots + j, PLANE, stride=slots), :] = jnp.where(code < 0, 0.0, value)
+
+    to_y.wait_send()
+
+    @pl.when(jnp.logical_not(yields))
+    def _():
+        to_x.wait_send()
 
 
 def on_device(cells_in, block_levels, send_x, send_y, layout, face_out, ghost_src):
@@ -355,33 +432,38 @@
     table = functools.partial(pltpu.VMEM, dtype=jnp.float32)
     out = pl.pallas_call(
         functools.partial(kernel, slots, gmax, moves, cap_out),
-        out_shape=pltpu.VMEM((FIELDS, cap_out, cells_in.shape[2]), jnp.float32),
+        out_shape=pltpu.VMEM((FIELDS * B * PLANE, LANES), jnp.float32),
         in_specs=[anywhere] * 7,
         out_specs=pl.BlockSpec(memory_space=pltpu.VMEM),
         scratch_shapes=[
-            table((3 * FIELDS * STRETCH, LANES)),
-            table((3, FIELDS, (B + 1) * PLANE, LANES)),
-            table((FIELDS, B * PLANE, LANES)),
+            table((2 * FIELDS * 4 * PLANE, LANES)),
             table((6 * slots, FACE_ROOM, LANES)),
             table((4 * gmax, FACE, LANES)),
             table((4, gmax, FACE, LANES)),
             table((6 * slots, FACE, LANES)),
-            table((slots, BLOCK, LANES)),
+            table((3 * FIELDS * STRETCH, LANES)),
+            table((3, FIELDS, (B + 1) * PLANE, LANES)),
+            table((FIELDS * B * PLANE, LANES)),
+            table((2, moves, FIELDS * INNER, LANES)),
+            table((2, moves, FIELDS * INNER, LANES)),
+            table((2, moves, BLOCK - FIELDS * INNER, LANES)),
+            table((2, moves, BLOCK - FIELDS * INNER, LANES)),
             table((2 * moves, BLOCK, LANES)),
-            table((2, moves, BLOCK, LANES)),
-            table((cap_out * BLOCK, LANES)),
             *(pltpu.SMEM(a.shape, jnp.int32) for a in small),
             pltpu.SemaphoreType.DMA((4,)),
             pltpu.SemaphoreType.DMA((4,)),
-            pltpu.SemaphoreType.DMA((2, FIELDS)),
-            pltpu.SemaphoreType.DMA((2, FIELDS)),
+            pltpu.SemaphoreType.DMA((2,)),
+            pltpu.SemaphoreType.DMA((2,)),
+            pltpu.SemaphoreType.DMA((2,)),
+            pltpu.SemaphoreType.DMA((2,)),
             pltpu.SemaphoreType.DMA((FIELDS,)),
             pltpu.SemaphoreType.DMA((len(small),)),
         ],
         compiler_params=pltpu.CompilerParams(collective_id=0, has_side_effects=True),
         name="section",
     )(lines, *small)
-    return out.transpose(1, 0, 2)
+    out = out.reshape(FIELDS, ROWS, slots, LANES).transpose(2, 0, 1, 3)
+    return out.reshape(slots, FIELDS, ROWS * LANES)[:cap_out]
 
 
 def solution(mesh):

time: 18.1 us -> 17 us (0.939)
  Pallas kernels: 15.9 us -> 14.7 us
    pallas_call x1, Pallas kernels: 15.9 us -> 14.7 us  [on_device(): pl.pallas_call(functools.partial(kernel, slots, gmax, moves, cap_out), ou...]
    slice x0 -> x1, local copies, waits for them, and re-layouts: none -> 0.75 us  [on_device(): return out.reshape(slots, FIELDS, ROWS * LANES)[:cap_out]]
    unnamed x1 -> x0, local copies, waits for them, and re-layouts: 0.73 us -> none
where the time goes in v1:
time: 17 us; the launch traced here: 16.8 us
  Pallas kernels  14.7 us (86%)
  between operations  1.3 us (8%)
  local copies, waits for them, and re-layouts  0.75 us (4%)
    pallas_call x1, Pallas kernels, on_device(): pl.pallas_call(functools.partial(kernel, slots, gmax, moves, cap_out), ou...  14.7 us
    slice x1, local copies, waits for them, and re-layouts, on_device(): return out.reshape(slots, FIELDS, ROWS * LANES)[:cap_out]  0.75 us

profile of v1, /device:TPU:0, one launch (start us, length us, event | category | flops | bytes accessed | tf_op | source)
XLA Modules:
  0.0 16.8 jit_solution(17058847595932132204)
XLA Ops:
  1.3 14.7 %section.1 = f32[640,128]{1,0:T(8,128)S(1)} custom-call(f32[5,128,128]{2,1,0:T(8,128)} %bitcast.11, s32[4]{0:T(128)} %levels_in.1, s32[1,1]{1,0:T(1,128)S(6)} %copy.10.send_x_in, s32[1,1]{1,0:T(1,128)S(6)} %copy.11.send_y_in, s32[1,3]{1,0:T(1,128)} %layout_in.1, s32[1,4,4]{2,1,0:T(4,128)} %face_out_in.1, s32[1,4,6]{2,1,0:T(4,128)} %ghost_src_in.1), custom_call_target="tpu_custom_call" | custom-call | tf_op jit(solution)/shard_map/section/pallas_call | solution.py:433
  16.0 0.7 %slice_bitcast_fusion = f32[3,5,4096]{2,0,1:T(4,128)} fusion(f32[4,5,32,128]{3,0,2,1:T(4,128)S(1)} %bitcast.10), kind=kLoop, calls=%fused_computation | loop fusion | bytes 491520 | tf_op jit(solution)/shard_map/slice | solution.py:466

commit v2 on v1

--- a/solution.py
+++ b/solution.py
@@ -124,17 +124,17 @@
     slots, gmax, moves, cap_out,
     cells, levels_in, send_x_in, send_y_in, layout_in, face_out_in, ghost_src_in,
     out,
-    edge, local_faces, far_faces, send_faces, ghosts, ext, flux, total,
+    edge, local_faces, far_faces, send_faces, ext, flux, total,
     early_out, early_in, late_out, late_in, arrived,
     levels, send_x, send_y, layout, face_out, ghost_src,
     face_send, face_recv, early_send, early_recv, late_send, late_recv, cell_sem, small_sem,
 ):
-    cell_copies = [
-        pltpu.make_async_copy(
-            cells.at[f], ext.at[pl.ds(f * STRETCH + 2 * PLANE, B * PLANE)], cell_sem.at[f]
-        )
-        for f in range(FIELDS)
-    ]
+    cell_copy = pltpu.make_async_copy(
+        cells,
+        ext.reshape(3 * FIELDS, STRETCH, LANES).at[pl.ds(0, FIELDS), pl.ds(2 * PLANE, B * PLANE)],
+        cell_sem,
+    )
+    cell_copy.start()
     small = (
         (face_out_in, face_out), (levels_in, levels), (ghost_src_in, ghost_src),
         (send_x_in, send_x), (send_y_in, send_y), (layout_in, layout),
@@ -143,8 +143,6 @@
         pltpu.make_async_copy(source, target, small_sem.at[i])
         for i, (source, target) in enumerate(small)
     ]
-    for copy in cell_copies + small_copies:
-        copy.start()
     n_x, n_y = lax.axis_size("bx"), lax.axis_size("by")
     i_x, i_y = lax.axis_index("bx"), lax.axis_index("by")
     beside = (
@@ -160,6 +158,8 @@
     barrier = pltpu.get_barrier_semaphore()
     for device in beside + partners:
         pl.semaphore_signal(barrier, inc=1, device_id=device, device_id_type=MESH)
+    for copy in small_copies:
+        copy.start()
 
     coords = [lax.broadcasted_iota(jnp.int32, (8, LANES), axis) for axis in (0, 1)]
 
@@ -170,8 +170,7 @@
         start = (axis * FIELDS + field) * STRETCH + plane * PLANE
         return pl.ds(pl.multiple_of(start, PLANE), PLANE)
 
-    for copy in cell_copies:
-        copy.wait()
+    cell_copy.wait()
     rim = (0, 1, B - 2, B - 1)
     for field in range(FIELDS):
         planes = [ext[ext_row(0, field, x + 2), :] for x in range(B)]
@@ -207,19 +206,20 @@
             send_faces[d, k] = local_face(face_out[0, d, k])
 
     pl.semaphore_wait(barrier, 6)
-    face_copies = [
-        pltpu.make_async_remote_copy(
-            src_ref=send_faces.at[d],
-            dst_ref=far_faces.at[pl.ds(d * gmax, gmax)],
-            send_sem=face_send.at[d],
-            recv_sem=face_recv.at[d],
+    def to_beside(d, source, target):
+        return pltpu.make_async_remote_copy(
+            src_ref=source,
+            dst_ref=target,
+            send_sem=face_send,
+            recv_sem=face_recv,
             device_id=beside[d],
             device_id_type=MESH,
         )
-        for d in range(4)
-    ]
-    for copy in face_copies:
-        copy.start()
+
+    for d in range(4):
+        to_beside(d, send_faces.at[d], far_faces.at[d]).start()
+    all_faces = to_beside(0, send_faces, far_faces)
+
     for field in range(FIELDS):
         planes = [ext[ext_row(0, field, x + 2), :] for x in range(B)]
         planes = swap_xy(planes, coords)
@@ -242,8 +242,8 @@
         return (
             0,
             1 + axis,
-            1 + lax.rem(axis + 1, 3),
-            1 + lax.rem(axis + 2, 3),
+            1 + (axis + 1) % 3,
+            1 + (axis + 2) % 3,
             4,
         )
 
@@ -321,10 +321,10 @@
 
     def to_partner(t, source, target, send_sem, recv_sem):
         return pltpu.make_async_remote_copy(
-            src_ref=source.at[t],
-            dst_ref=target.at[t],
-            send_sem=send_sem.at[t],
-            recv_sem=recv_sem.at[t],
+            src_ref=source,
+            dst_ref=target,
+            send_sem=send_sem,
+            recv_sem=recv_sem,
             device_id=partners[t],
             device_id_type=MESH,
         )
@@ -333,63 +333,67 @@
         for field in range(FIELDS):
             first, second = (half_lines(slot, field, half) for half in range(HALVES))
             early_out[t, m, pl.ds(field * INNER, INNER), :] = exchanged(second, first, outof, -1)
-    early_copies = [to_partner(t, early_out, early_in, early_send, early_recv) for t in range(2)]
-    for copy in reversed(early_copies):
-        copy.start()
-
-    for copy in face_copies:
-        copy.wait()
-    for axis in range(3):
+    for t in (1, 0):
+        to_partner(t, early_out.at[t], early_in.at[t], early_send, early_recv).start()
+    all_early = to_partner(0, early_out, early_in, early_send, early_recv)
+
+    all_faces.wait()
+    def put_ghosts(axis):
         for side in range(2):
             for b in range(slots):
                 code = ghost_src[0, b, axis * 2 + side]
-                near = local_face(jnp.minimum(code, 6 * slots - 1))
-                far = far_faces[jnp.maximum(code - 6 * slots, 0)]
-                ghost = b * 6 + axis * 2 + side
-                ghosts[ghost] = jnp.where(code < 6 * slots, near, far)
+                near = jnp.minimum(code, 6 * slots - 1)
+                far = jnp.maximum(code - 6 * slots, 0)
+                d, k = lax.div(far, gmax), lax.rem(far, gmax)
                 for layer in range(2):
                     plane = 1 - layer if side == 0 else B + 2 + layer
                     for half in range(HALVES):
+                        lines = pl.ds(layer * 2 + half, FIELDS, stride=4)
                         start = axis * FIELDS * STRETCH + plane * PLANE + half * slots + b
-                        ext[pl.ds(start, FIELDS, stride=STRETCH), :] = ghosts[
-                            ghost, pl.ds(layer * 2 + half, FIELDS, stride=4), :
-                        ]
-
-    def outer(axis, carry):
+                        ext[pl.ds(start, FIELDS, stride=STRETCH), :] = jnp.where(
+                            code < 6 * slots, local_faces[near, lines, :], far_faces[d, k, lines, :]
+                        )
+
+    for axis in (2, 1, 0):
+        put_ghosts(axis)
         sweep(axis, 1, 3)
         sweep(axis, B, B + 2)
-        return carry
-
-    lax.fori_loop(0, 3, outer, 0)
 
     for field in range(FIELDS):
         planes = changes(field, (0, 1, B - 1, B))
         for x in range(B):
             total[total_row(field, x), :] = total[total_row(field, x), :] - ratio * planes[x]
 
-    for t, m, slot in reversed(lists):
-        for field in range(FIELDS):
-            first, second = (half_lines(slot, field, half) for half in range(HALVES))
-            late_out[t, m, pl.ds(field * INNER, INNER), :] = exchanged(first, second, into, 1)
-            for i, x in enumerate((0, B - 2)):
-                at = FIELDS * INNER + field * 8 + i * 4
-                late_out[t, m, pl.ds(at, 4), :] = edge_lines(slot, field, x)
-    to_x, to_y = (to_partner(t, late_out, late_in, late_send, late_recv) for t in range(2))
+    def fill_late(axis):
+        for t, m, slot in lists:
+            if t != axis:
+                continue
+            for field in range(FIELDS):
+                first, second = (half_lines(slot, field, half) for half in range(HALVES))
+                late_out[t, m, pl.ds(field * INNER, INNER), :] = exchanged(first, second, into, 1)
+                for i, x in enumerate((0, B - 2)):
+                    at = FIELDS * INNER + field * 8 + i * 4
+                    late_out[t, m, pl.ds(at, 4), :] = edge_lines(slot, field, x)
+
+    to_x, to_y = (
+        to_partner(t, late_out.at[t], late_in.at[t], late_send.at[t], late_recv.at[t]) for t in range(2)
+    )
     yields = i_y >= n_y - n_y // 4
+    fill_late(1)
 
     @pl.when(jnp.logical_not(yields))
     def _():
         to_y.start()
-        to_x.start()
+
+    fill_late(0)
+    to_x.start()
 
     @pl.when(yields)
     def _():
-        to_x.start()
         to_x.wait_send()
         to_y.start()
 
-    for t in range(2):
-        early_copies[t].wait()
+    all_early.wait()
     for t in range(2):
         (to_x, to_y)[t].wait_recv()
         for m in range(moves):
@@ -438,9 +442,8 @@
         scratch_shapes=[
             table((2 * FIELDS * 4 * PLANE, LANES)),
             table((6 * slots, FACE_ROOM, LANES)),
-            table((4 * gmax, FACE, LANES)),
             table((4, gmax, FACE, LANES)),
-            table((6 * slots, FACE, LANES)),
+            table((4, gmax, FACE, LANES)),
             table((3 * FIELDS * STRETCH, LANES)),
             table((3, FIELDS, (B + 1) * PLANE, LANES)),
             table((FIELDS * B * PLANE, LANES)),
@@ -450,13 +453,13 @@
             table((2, moves, BLOCK - FIELDS * INNER, LANES)),
             table((2 * moves, BLOCK, LANES)),
             *(pltpu.SMEM(a.shape, jnp.int32) for a in small),
-            pltpu.SemaphoreType.DMA((4,)),
-            pltpu.SemaphoreType.DMA((4,)),
+            pltpu.SemaphoreType.DMA(()),
+            pltpu.SemaphoreType.DMA(()),
+            pltpu.SemaphoreType.DMA(()),
+            pltpu.SemaphoreType.DMA(()),
             pltpu.SemaphoreType.DMA((2,)),
             pltpu.SemaphoreType.DMA((2,)),
-            pltpu.SemaphoreType.DMA((2,)),
-            pltpu.SemaphoreType.DMA((2,)),
-            pltpu.SemaphoreType.DMA((FIELDS,)),
+            pltpu.SemaphoreType.DMA(()),
             pltpu.SemaphoreType.DMA((len(small),)),
         ],
         compiler_params=pltpu.CompilerParams(collective_id=0, has_side_effects=True),

time: 17 us -> 16.4 us (0.965)
  Pallas kernels: 14.7 us -> 14.1 us
    pallas_call x1, Pallas kernels: 14.7 us -> 14.1 us  [on_device(): pl.pallas_call(functools.partial(kernel, slots, gmax, moves, cap_out), ou...]
where the time goes in v2:
time: 16.4 us; the launch traced here: 16.2 us
  Pallas kernels  14.1 us (86%)
  between operations  1.3 us (8%)
  local copies, waits for them, and re-layouts  0.75 us (5%)
    pallas_call x1, Pallas kernels, on_device(): pl.pallas_call(functools.partial(kernel, slots, gmax, moves, cap_out), ou...  14.1 us
    slice x1, local copies, waits for them, and re-layouts, on_device(): return out.reshape(slots, FIELDS, ROWS * LANES)[:cap_out]  0.75 us

profile of v2, /device:TPU:0, one launch (start us, length us, event | category | flops | bytes accessed | tf_op | source)
XLA Modules:
  0.0 16.2 jit_solution(17319864689225221916)
XLA Ops:
  1.3 14.1 %section.1 = f32[640,128]{1,0:T(8,128)S(1)} custom-call(f32[5,128,128]{2,1,0:T(8,128)} %bitcast.11, s32[4]{0:T(128)} %levels_in.1, s32[1,1]{1,0:T(1,128)S(6)} %copy.10.send_x_in, s32[1,1]{1,0:T(1,128)S(6)} %copy.11.send_y_in, s32[1,3]{1,0:T(1,128)} %layout_in.1, s32[1,4,4]{2,1,0:T(4,128)} %face_out_in.1, s32[1,4,6]{2,1,0:T(4,128)} %ghost_src_in.1), custom_call_target="tpu_custom_call" | custom-call | tf_op jit(solution)/shard_map/section/pallas_call | solution.py:437
  15.4 0.7 %slice_bitcast_fusion = f32[3,5,4096]{2,0,1:T(4,128)} fusion(f32[4,5,32,128]{3,0,2,1:T(4,128)S(1)} %bitcast.10), kind=kLoop, calls=%fused_computation | loop fusion | bytes 491520 | tf_op jit(solution)/shard_map/slice | solution.py:469

commit v3 on v2

--- a/solution.py
+++ b/solution.py
@@ -122,19 +122,13 @@
 
 def kernel(
     slots, gmax, moves, cap_out,
-    cells, levels_in, send_x_in, send_y_in, layout_in, face_out_in, ghost_src_in,
+    cells, levels_in, send_x_in, send_y_in, layout_in, face_out_in, ghost_src_in, first_in,
     out,
     edge, local_faces, far_faces, send_faces, ext, flux, total,
     early_out, early_in, late_out, late_in, arrived,
     levels, send_x, send_y, layout, face_out, ghost_src,
-    face_send, face_recv, early_send, early_recv, late_send, late_recv, cell_sem, small_sem,
+    face_send, face_recv, early_send, early_recv, late_send, late_recv, small_sem,
 ):
-    cell_copy = pltpu.make_async_copy(
-        cells,
-        ext.reshape(3 * FIELDS, STRETCH, LANES).at[pl.ds(0, FIELDS), pl.ds(2 * PLANE, B * PLANE)],
-        cell_sem,
-    )
-    cell_copy.start()
     small = (
         (face_out_in, face_out), (levels_in, levels), (ghost_src_in, ghost_src),
         (send_x_in, send_x), (send_y_in, send_y), (layout_in, layout),
@@ -143,6 +137,8 @@
         pltpu.make_async_copy(source, target, small_sem.at[i])
         for i, (source, target) in enumerate(small)
     ]
+    for copy in small_copies:
+        copy.start()
     n_x, n_y = lax.axis_size("bx"), lax.axis_size("by")
     i_x, i_y = lax.axis_index("bx"), lax.axis_index("by")
     beside = (
@@ -158,8 +154,6 @@
     barrier = pltpu.get_barrier_semaphore()
     for device in beside + partners:
         pl.semaphore_signal(barrier, inc=1, device_id=device, device_id_type=MESH)
-    for copy in small_copies:
-        copy.start()
 
     coords = [lax.broadcasted_iota(jnp.int32, (8, LANES), axis) for axis in (0, 1)]
 
@@ -170,10 +164,11 @@
         start = (axis * FIELDS + field) * STRETCH + plane * PLANE
         return pl.ds(pl.multiple_of(start, PLANE), PLANE)
 
-    cell_copy.wait()
     rim = (0, 1, B - 2, B - 1)
     for field in range(FIELDS):
-        planes = [ext[ext_row(0, field, x + 2), :] for x in range(B)]
+        planes = [cells[field, row(x), :] for x in range(B)]
+        for x in range(B):
+            ext[ext_row(0, field, x + 2), :] = planes[x]
         planes = swap_xy(planes, coords)
         for i, y in enumerate(rim):
             edge[row(field * 4 + i), :] = planes[y]
@@ -190,8 +185,7 @@
                     for half in range(HALVES):
                         target = (axis * 2 + side) * FACE_ROOM + field * 4 + layer * 2 + half
                         if axis == 0:
-                            at = field * STRETCH + (rim[nth] + 2) * PLANE + half * slots
-                            value = ext[pl.ds(at, slots), :]
+                            value = cells[field, pl.ds(rim[nth] * PLANE + half * slots, slots), :]
                         else:
                             at = (((axis - 1) * FIELDS + field) * 4 + nth) * PLANE + half * slots
                             value = edge[pl.ds(at, slots), :]
@@ -430,15 +424,28 @@
     moves = send_x.shape[1]
     cap_out = layout.shape[1]
     small = (block_levels, send_x, send_y, layout, face_out, ghost_src)
-    anywhere = pl.BlockSpec(memory_space=pltpu.HBM)
+    near = pl.BlockSpec(memory_space=pltpu.VMEM)
+    far = pl.BlockSpec(memory_space=pltpu.HBM)
+    held = functools.partial(pltpu.with_memory_space_constraint, memory_space=pltpu.VMEM)
     lines = cells_in.reshape(slots, FIELDS, ROWS, LANES).transpose(1, 2, 0, 3)
     lines = lines.reshape(FIELDS, ROWS * slots, LANES)
     table = functools.partial(pltpu.VMEM, dtype=jnp.float32)
+
+    def mark(target):
+        target[...] = jnp.zeros_like(target)
+
+    first = pl.pallas_call(
+        mark,
+        out_shape=pltpu.VMEM((PLANE, LANES), jnp.float32),
+        out_specs=near,
+        cost_estimate=pl.CostEstimate(flops=100000000, bytes_accessed=0, transcendentals=0),
+        name="first",
+    )()
     out = pl.pallas_call(
         functools.partial(kernel, slots, gmax, moves, cap_out),
         out_shape=pltpu.VMEM((FIELDS * B * PLANE, LANES), jnp.float32),
-        in_specs=[anywhere] * 7,
-        out_specs=pl.BlockSpec(memory_space=pltpu.VMEM),
+        in_specs=[near, *[far] * 6, near],
+        out_specs=near,
         scratch_shapes=[
             table((2 * FIELDS * 4 * PLANE, LANES)),
             table((6 * slots, FACE_ROOM, LANES)),
@@ -459,12 +466,11 @@
             pltpu.SemaphoreType.DMA(()),
             pltpu.SemaphoreType.DMA((2,)),
             pltpu.SemaphoreType.DMA((2,)),
-            pltpu.SemaphoreType.DMA(()),
             pltpu.SemaphoreType.DMA((len(small),)),
         ],
         compiler_params=pltpu.CompilerParams(collective_id=0, has_side_effects=True),
         name="section",
-    )(lines, *small)
+    )(held(lines), *small, held(first))
     out = out.reshape(FIELDS, ROWS, slots, LANES).transpose(2, 0, 1, 3)
     return out.reshape(slots, FIELDS, ROWS * LANES)[:cap_out]
 

time: 16.4 us -> 15.7 us (0.957)
  Pallas kernels: 14.1 us -> 13.4 us
    pallas_call x1, Pallas kernels: 14.1 us -> 13.4 us  [on_device(): pl.pallas_call(functools.partial(kernel, slots, gmax, moves, cap_out), ou...]
where the time goes in v3:
time: 15.7 us; the launch traced here: 15.6 us
  Pallas kernels  13.4 us (85%)
  between operations  1.37 us (9%)
  local copies, waits for them, and re-layouts  0.75 us (5%)
    pallas_call x1, Pallas kernels, on_device(): pl.pallas_call(functools.partial(kernel, slots, gmax, moves, cap_out), ou...  13.4 us
    slice x1, local copies, waits for them, and re-layouts, on_device(): return out.reshape(slots, FIELDS, ROWS * LANES)[:cap_out]  0.75 us

profile of v3, /device:TPU:0, one launch (start us, length us, event | category | flops | bytes accessed | tf_op | source)
XLA Modules:
  0.0 15.6 jit_solution(9826219203132258748)
XLA Ops:
  0.0 0.0 copy-start
  1.4 0.0 copy-done
  1.4 13.4 %section.1 = f32[640,128]{1,0:T(8,128)S(1)} custom-call(f32[5,128,128]{2,1,0:T(8,128)S(1)} %bitcast.11, s32[4]{0:T(128)} %levels_in.1, s32[1,1]{1,0:T(1,128)S(6)} %copy.10.send_x_in, s32[1,1]{1,0:T(1,128)S(6)} %copy.11.send_y_in, s32[1,3]{1,0:T(1,128)} %layout_in.1, s32[1,4,4]{2,1,0:T(4,128)} %face_out_in.1, s32[1,4,6]{2,1,0:T(4,128)} %ghost_src_in.1, ...), custom_call_target="tpu_custom_call" | custom-call | tf_op jit(solution)/shard_map/section/pallas_call | solution.py:444
  14.8 0.7 %slice_bitcast_fusion = f32[3,5,4096]{2,0,1:T(4,128)} fusion(f32[4,5,32,128]{3,0,2,1:T(4,128)S(1)} %bitcast.10), kind=kLoop, calls=%fused_computation | loop fusion | bytes 491520 | tf_op jit(solution)/shard_map/slice | solution.py:475
  (1 shorter events, 0.0 us)
Async XLA Ops:
  0.0 1.4 %copy-start = (f32[4,5,4096]{2,0,1:T(4,128)S(1)}, f32[4,5,4096]{2,0,1:T(4,128)}, u32[]{:S(2)}) copy-start(f32[4,5,4096]{2,0,1:T(4,128)} %param.7) | copy-start | bytes 983044

commit v4 on v3

--- a/solution.py
+++ b/solution.py
@@ -127,7 +127,7 @@
     edge, local_faces, far_faces, send_faces, ext, flux, total,
     early_out, early_in, late_out, late_in, arrived,
     levels, send_x, send_y, layout, face_out, ghost_src,
-    face_send, face_recv, early_send, early_recv, late_send, late_recv, small_sem,
+    face_send, face_recv, early_send, early_recv, late_send, late_recv, small_sem, ready,
 ):
     small = (
         (face_out_in, face_out), (levels_in, levels), (ghost_src_in, ghost_src),
@@ -152,8 +152,24 @@
         {"by": lax.rem(i_y + n_y // 2, n_y)},
     )
     barrier = pltpu.get_barrier_semaphore()
-    for device in beside + partners:
-        pl.semaphore_signal(barrier, inc=1, device_id=device, device_id_type=MESH)
+    first_row, last_row = i_y == 0, i_y == n_y - 1
+    upper = (i_x >= n_x // 2, i_y >= n_y // 2)
+
+    def greet(semaphore, device):
+        pl.semaphore_signal(semaphore, inc=1, device_id=device, device_id_type=MESH)
+
+    for device in beside[:2] + beside[3:]:
+        greet(barrier, device)
+
+    @pl.when(jnp.logical_not(last_row))
+    def _():
+        greet(barrier, beside[2])
+
+    for t in range(2):
+
+        @pl.when(jnp.logical_not(upper[t]))
+        def _(t=t):
+            greet(barrier, partners[t])
 
     coords = [lax.broadcasted_iota(jnp.int32, (8, LANES), axis) for axis in (0, 1)]
 
@@ -199,7 +215,8 @@
         for k in range(gmax):
             send_faces[d, k] = local_face(face_out[0, d, k])
 
-    pl.semaphore_wait(barrier, 6)
+    expected = 4 - lax.div(n_y - i_y, n_y) + sum(lax.div(i, n // 2) for i, n in ((i_x, n_x), (i_y, n_y)))
+    pl.semaphore_wait(barrier, expected)
     def to_beside(d, source, target):
         return pltpu.make_async_remote_copy(
             src_ref=source,
@@ -210,8 +227,26 @@
             device_id_type=MESH,
         )
 
-    for d in range(4):
+    def send_face(d):
         to_beside(d, send_faces.at[d], far_faces.at[d]).start()
+
+    for d in range(3):
+        send_face(d)
+
+    @pl.when(jnp.logical_not(first_row))
+    def _():
+        send_face(3)
+
+    @pl.when(last_row)
+    def _():
+        greet(ready.at[0], beside[2])
+
+    for t in range(2):
+
+        @pl.when(upper[t])
+        def _(t=t):
+            greet(ready.at[1 + t], partners[t])
+
     all_faces = to_beside(0, send_faces, far_faces)
 
     for field in range(FIELDS):
@@ -285,6 +320,11 @@
         for x in range(B):
             total[total_row(field, x), :] = total[total_row(field, x), :] - ratio * planes[x]
 
+    @pl.when(first_row)
+    def _():
+        pl.semaphore_wait(ready.at[0], 1)
+        send_face(3)
+
     lane = lax.broadcasted_iota(jnp.int32, (INNER, LANES), 1)
 
     def any_of(spans):
@@ -328,6 +368,11 @@
             first, second = (half_lines(slot, field, half) for half in range(HALVES))
             early_out[t, m, pl.ds(field * INNER, INNER), :] = exchanged(second, first, outof, -1)
     for t in (1, 0):
+
+        @pl.when(jnp.logical_not(upper[t]))
+        def _(t=t):
+            pl.semaphore_wait(ready.at[1 + t], 1)
+
         to_partner(t, early_out.at[t], early_in.at[t], early_send, early_recv).start()
     all_early = to_partner(0, early_out, early_in, early_send, early_recv)
 
@@ -372,21 +417,10 @@
     to_x, to_y = (
         to_partner(t, late_out.at[t], late_in.at[t], late_send.at[t], late_recv.at[t]) for t in range(2)
     )
-    yields = i_y >= n_y - n_y // 4
     fill_late(1)
-
-    @pl.when(jnp.logical_not(yields))
-    def _():
-        to_y.start()
-
+    to_y.start()
     fill_late(0)
     to_x.start()
-
-    @pl.when(yields)
-    def _():
-        to_x.wait_send()
-        to_y.start()
-
     all_early.wait()
     for t in range(2):
         (to_x, to_y)[t].wait_recv()
@@ -412,10 +446,7 @@
             out[pl.ds(k * slots + j, PLANE, stride=slots), :] = jnp.where(code < 0, 0.0, value)
 
     to_y.wait_send()
-
-    @pl.when(jnp.logical_not(yields))
-    def _():
-        to_x.wait_send()
+    to_x.wait_send()
 
 
 def on_device(cells_in, block_levels, send_x, send_y, layout, face_out, ghost_src):
@@ -467,6 +498,7 @@
             pltpu.SemaphoreType.DMA((2,)),
             pltpu.SemaphoreType.DMA((2,)),
             pltpu.SemaphoreType.DMA((len(small),)),
+            pltpu.SemaphoreType.REGULAR((3,)),
         ],
         compiler_params=pltpu.CompilerParams(collective_id=0, has_side_effects=True),
         name="section",

time: 15.7 us -> 15.5 us (0.987)
  Pallas kernels: 13.4 us -> 13.2 us
    pallas_call x1, Pallas kernels: 13.4 us -> 13.2 us  [on_device(): pl.pallas_call(functools.partial(kernel, slots, gmax, moves, cap_out), ou...]
where the time goes in v4:
time: 15.5 us; the launch traced here: 15.3 us
  Pallas kernels  13.2 us (85%)
  between operations  1.37 us (9%)
  local copies, waits for them, and re-layouts  0.75 us (5%)
    pallas_call x1, Pallas kernels, on_device(): pl.pallas_call(functools.partial(kernel, slots, gmax, moves, cap_out), ou...  13.2 us
    slice x1, local copies, waits for them, and re-layouts, on_device(): return out.reshape(slots, FIELDS, ROWS * LANES)[:cap_out]  0.75 us

profile of v4, /device:TPU:0, one launch (start us, length us, event | category | flops | bytes accessed | tf_op | source)
XLA Modules:
  0.0 15.3 jit_solution(12909588438753609304)
XLA Ops:
  0.0 0.0 copy-start
  1.4 0.0 copy-done
  1.4 13.2 %section.1 = f32[640,128]{1,0:T(8,128)S(1)} custom-call(f32[5,128,128]{2,1,0:T(8,128)S(1)} %bitcast.11, s32[4]{0:T(128)} %levels_in.1, s32[1,1]{1,0:T(1,128)S(6)} %copy.10.send_x_in, s32[1,1]{1,0:T(1,128)S(6)} %copy.11.send_y_in, s32[1,3]{1,0:T(1,128)} %layout_in.1, s32[1,4,4]{2,1,0:T(4,128)} %face_out_in.1, s32[1,4,6]{2,1,0:T(4,128)} %ghost_src_in.1, ...), custom_call_target="tpu_custom_call" | custom-call | tf_op jit(solution)/shard_map/section/pallas_call | solution.py:475
  14.5 0.7 %slice_bitcast_fusion = f32[3,5,4096]{2,0,1:T(4,128)} fusion(f32[4,5,32,128]{3,0,2,1:T(4,128)S(1)} %bitcast.10), kind=kLoop, calls=%fused_computation | loop fusion | bytes 491520 | tf_op jit(solution)/shard_map/slice | solution.py:507
  (1 shorter events, 0.0 us)
Async XLA Ops:
  0.0 1.4 %copy-start = (f32[4,5,4096]{2,0,1:T(4,128)S(1)}, f32[4,5,4096]{2,0,1:T(4,128)}, u32[]{:S(2)}) copy-start(f32[4,5,4096]{2,0,1:T(4,128)} %param.7) | copy-start | bytes 983044

commit v5 on v4

--- a/solution.py
+++ b/solution.py
@@ -422,6 +422,13 @@
     fill_late(0)
     to_x.start()
     all_early.wait()
+    swapped = functools.reduce(jnp.logical_or, into)
+    for t in range(2):
+        for m in range(moves):
+            for field in range(FIELDS):
+                early = early_in[t, m, pl.ds(field * INNER, INNER), :]
+                at = field * ROWS + 2 * HALVES
+                arrived[t * moves + m, pl.ds(at, INNER, stride=HALVES), :] = exchanged(early, early, into, 1)
     for t in range(2):
         (to_x, to_y)[t].wait_recv()
         for m in range(moves):
@@ -430,7 +437,8 @@
                 early = early_in[t, m, pl.ds(field * INNER, INNER), :]
                 late = late_in[t, m, pl.ds(field * INNER, INNER), :]
                 at = field * ROWS + 2 * HALVES
-                arrived[block, pl.ds(at, INNER, stride=HALVES), :] = exchanged(late, early, into, 1)
+                ahead = arrived[block, pl.ds(at, INNER, stride=HALVES), :]
+                arrived[block, pl.ds(at, INNER, stride=HALVES), :] = jnp.where(swapped, ahead, late)
                 arrived[block, pl.ds(at + 1, INNER, stride=HALVES), :] = exchanged(early, late, outof, -1)
                 for i, x in enumerate((0, B - 2)):
                     at = FIELDS * INNER + field * 8 + i * 4

time: 15.5 us -> 15.4 us (level)
  no operation moved by 1% of the time
where the time goes in v5:
time: 15.4 us; the launch traced here: 15.2 us
  Pallas kernels  13.1 us (85%)
  between operations  1.37 us (9%)
  local copies, waits for them, and re-layouts  0.75 us (5%)
    pallas_call x1, Pallas kernels, on_device(): pl.pallas_call(functools.partial(kernel, slots, gmax, moves, cap_out), ou...  13.1 us
    slice x1, local copies, waits for them, and re-layouts, on_device(): return out.reshape(slots, FIELDS, ROWS * LANES)[:cap_out]  0.75 us

profile of v5, /device:TPU:0, one launch (start us, length us, event | category | flops | bytes accessed | tf_op | source)
XLA Modules:
  0.0 15.2 jit_solution(1362184180983363308)
XLA Ops:
  0.0 0.0 copy-start
  1.4 0.0 copy-done
  1.4 13.1 %section.1 = f32[640,128]{1,0:T(8,128)S(1)} custom-call(f32[5,128,128]{2,1,0:T(8,128)S(1)} %bitcast.11, s32[4]{0:T(128)} %levels_in.1, s32[1,1]{1,0:T(1,128)S(6)} %copy.10.send_x_in, s32[1,1]{1,0:T(1,128)S(6)} %copy.11.send_y_in, s32[1,3]{1,0:T(1,128)} %layout_in.1, s32[1,4,4]{2,1,0:T(4,128)} %face_out_in.1, s32[1,4,6]{2,1,0:T(4,128)} %ghost_src_in.1, ...), custom_call_target="tpu_custom_call" | custom-call | tf_op jit(solution)/shard_map/section/pallas_call | solution.py:483
  14.5 0.7 %slice_bitcast_fusion = f32[3,5,4096]{2,0,1:T(4,128)} fusion(f32[4,5,32,128]{3,0,2,1:T(4,128)S(1)} %bitcast.10), kind=kLoop, calls=%fused_computation | loop fusion | bytes 491520 | tf_op jit(solution)/shard_map/slice | solution.py:515
  (1 shorter events, 0.0 us)
Async XLA Ops:
  0.0 1.4 %copy-start = (f32[4,5,4096]{2,0,1:T(4,128)S(1)}, f32[4,5,4096]{2,0,1:T(4,128)}, u32[]{:S(2)}) copy-start(f32[4,5,4096]{2,0,1:T(4,128)} %param.7) | copy-start | bytes 983044

commit v6 on v5

--- a/solution.py
+++ b/solution.py
@@ -415,7 +415,7 @@
                     late_out[t, m, pl.ds(at, 4), :] = edge_lines(slot, field, x)
 
     to_x, to_y = (
-        to_partner(t, late_out.at[t], late_in.at[t], late_send.at[t], late_recv.at[t]) for t in range(2)
+        to_partner(t, late_out.at[t], late_in.at[t], late_send, late_recv.at[t]) for t in range(2)
     )
     fill_late(1)
     to_y.start()
@@ -453,8 +453,7 @@
             value = jnp.where(code < slots, own, arrived[theirs, pl.ds(k, PLANE), :])
             out[pl.ds(k * slots + j, PLANE, stride=slots), :] = jnp.where(code < 0, 0.0, value)
 
-    to_y.wait_send()
-    to_x.wait_send()
+    to_partner(0, late_out, late_in, late_send, late_recv.at[0]).wait_send()
 
 
 def on_device(cells_in, block_levels, send_x, send_y, layout, face_out, ghost_src):
@@ -503,7 +502,7 @@
             pltpu.SemaphoreType.DMA(()),
             pltpu.SemaphoreType.DMA(()),
             pltpu.SemaphoreType.DMA(()),
-            pltpu.SemaphoreType.DMA((2,)),
+            pltpu.SemaphoreType.DMA(()),
             pltpu.SemaphoreType.DMA((2,)),
             pltpu.SemaphoreType.DMA((len(small),)),
             pltpu.SemaphoreType.REGULAR((3,)),

time: 15.4 us -> 15.4 us (level)
  no operation moved by 1% of the time
where the time goes in v6:
time: 15.4 us; the launch traced here: 15.2 us
  Pallas kernels  13.1 us (85%)
  between operations  1.37 us (9%)
  local copies, waits for them, and re-layouts  0.75 us (5%)
    pallas_call x1, Pallas kernels, on_device(): pl.pallas_call(functools.partial(kernel, slots, gmax, moves, cap_out), ou...  13.1 us
    slice x1, local copies, waits for them, and re-layouts, on_device(): return out.reshape(slots, FIELDS, ROWS * LANES)[:cap_out]  0.75 us

profile of v6, /device:TPU:0, one launch (start us, length us, event | category | flops | bytes accessed | tf_op | source)
XLA Modules:
  0.0 15.2 jit_solution(1564177456500239602)
XLA Ops:
  0.0 0.0 copy-start
  1.4 0.0 copy-done
  1.4 13.1 %section.1 = f32[640,128]{1,0:T(8,128)S(1)} custom-call(f32[5,128,128]{2,1,0:T(8,128)S(1)} %bitcast.11, s32[4]{0:T(128)} %levels_in.1, s32[1,1]{1,0:T(1,128)S(6)} %copy.10.send_x_in, s32[1,1]{1,0:T(1,128)S(6)} %copy.11.send_y_in, s32[1,3]{1,0:T(1,128)} %layout_in.1, s32[1,4,4]{2,1,0:T(4,128)} %face_out_in.1, s32[1,4,6]{2,1,0:T(4,128)} %ghost_src_in.1, ...), custom_call_target="tpu_custom_call" | custom-call | tf_op jit(solution)/shard_map/section/pallas_call | solution.py:482
  14.5 0.7 %slice_bitcast_fusion = f32[3,5,4096]{2,0,1:T(4,128)} fusion(f32[4,5,32,128]{3,0,2,1:T(4,128)S(1)} %bitcast.10), kind=kLoop, calls=%fused_computation | loop fusion | bytes 491520 | tf_op jit(solution)/shard_map/slice | solution.py:514
  (1 shorter events, 0.0 us)
Async XLA Ops:
  0.0 1.4 %copy-start = (f32[4,5,4096]{2,0,1:T(4,128)S(1)}, f32[4,5,4096]{2,0,1:T(4,128)}, u32[]{:S(2)}) copy-start(f32[4,5,4096]{2,0,1:T(4,128)} %param.7) | copy-start | bytes 983044
